TPU v7x, 256 devices: a whole 4x4x8 slice. The times are simulated.
256 devices in a mesh: row: 4 (over x), col: 16 (over y, z_lo), gz: 4 (over z_hi, core).
Axes of the slice: x: 4, y: 4, z: 8 (z_hi: 2, z_lo: 4; z = z_hi * 4 + z_lo), core: 2. Of those that a mesh axis runs over, the one named last changes fastest.
Arguments:
- volume_field: bfloat16 [128, 32, 128, 512], P(None, 'row', 'col', 'gz'), may hold values from -6 to 6
- volume_load: bfloat16 [128, 32, 128, 512], P(None, 'row', 'col', 'gz'), may hold values from -6 to 6
- coefficient: float32 [32, 128, 512], P('row', 'col', 'gz'), may hold values from 0.25 to 2
- surface_block: bfloat16 [1024, 262144], P('row', 'col'), may hold values from -0.015625 to 0.015625
- trace_cell: int32 [4, 16, 4, 1024], P('row', 'col', 'gz'), may hold values from 0 to 8191, as said below
- flux_cell: int32 [4, 16, 4, 4], P('row', 'col', 'gz'), may hold values from 0 to 8191, as said below
Outputs:
- new_field: bfloat16 [128, 32, 128, 512], P(None, 'row', 'col', 'gz')
- surface_flux: float32 [128, 1024], P('gz', ('row', 'col'))
Inputs may be any that keep to these rules, and one draw needn't show every extreme that they name: `trace_cell`: within each device's 1024 entries, entry values are local cell numbers, one from each aligned run of 8 consecutive cells, in a permuted order; the first and last cells of the block are always chosen. `flux_cell`: within each device's 4 entries, entry values are local cell numbers, one from each aligned run of 2048 consecutive cells, in a permuted order; the first and last cells of the block are always chosen.
All inputs are finite; a program needn't handle non-finite values.
Results may differ from a plain program's by a relative error of at most 0.0032.
Values may be sent and summed in bfloat16 or wider, within the bound.
A program may use at most 128 MiB of HBM per device.

v0:
```python
import jax
import jax.numpy as jnp
from jax import lax
from jax.sharding import PartitionSpec as P

OMEGA = 0.8


def padded_2(array, sides, width):
    for axis, dim in sides:
        peers, length = (lax.axis_size(axis), array.shape[dim])
        up = [(i, (i + 1) % peers) for i in range(peers - 1)]
        down = [(j, i) for i, j in up]
        last = lax.slice_in_dim(array, length - width, length, axis=dim)
        first = lax.slice_in_dim(array, 0, width, axis=dim)
        before = lax.ppermute(last, axis, up)
        after = lax.ppermute(first, axis, down)
        array = jnp.concatenate([before, array, after], axis=dim)
    return array


def relax(current, source, diagonal):
    padded = padded_2(current, (("row", 1), ("col", 2), ("gz", 3)), 1).astype(jnp.float32)
    centre = current.astype(jnp.float32)
    beside = padded[:, 2:, 1:-1, 1:-1] + padded[:, :-2, 1:-1, 1:-1]
    beside = beside + padded[:, 1:-1, 2:, 1:-1] + padded[:, 1:-1, :-2, 1:-1]
    beside = beside + padded[:, 1:-1, 1:-1, 2:] + padded[:, 1:-1, 1:-1, :-2]
    return (centre + OMEGA * (source - (diagonal * centre - beside)) / diagonal).astype(
        jnp.bfloat16
    )


def per_device(volume_field, volume_load, coefficient, surface_block, trace_cell, flux_cell):
    side_count, first_span, second_span, third_span = volume_field.shape
    cell_count = first_span * second_span * third_span
    slot_count = trace_cell.shape[3]
    flux_slots = flux_cell.shape[3]
    side_group = side_count // lax.axis_size("gz")
    flat_field = volume_field.reshape(side_count, cell_count)
    picker = (
        lax.broadcasted_iota(jnp.int32, (cell_count, slot_count), 0)
        == trace_cell.reshape(1, slot_count)
    ).astype(jnp.bfloat16)
    trace_values = jnp.dot(flat_field, picker, preferred_element_type=jnp.float32).astype(
        jnp.bfloat16
    )
    layer_index = lax.axis_index("gz")
    chosen = lax.dynamic_slice_in_dim(
        lax.all_gather(trace_values, ("row", "gz"), axis=1, tiled=True),
        layer_index * side_group,
        side_group,
        0,
    )
    partial_flux = lax.dot_general(
        chosen, surface_block, (((1,), (1,)), ((), ())), preferred_element_type=jnp.float32
    )
    surface_flux = lax.psum_scatter(partial_flux, "col", scatter_dimension=1, tiled=True)
    owned_flux = lax.all_to_all(surface_flux, "gz", split_axis=1, concat_axis=0, tiled=True)
    placer = (
        flux_cell.reshape(flux_slots, 1)
        == lax.broadcasted_iota(jnp.int32, (flux_slots, cell_count), 1)
    ).astype(jnp.float32)
    placed = jnp.dot(
        owned_flux, placer, precision=lax.Precision.HIGHEST, preferred_element_type=jnp.float32
    )
    source = volume_load.astype(jnp.float32) + placed.reshape(
        side_count, first_span, second_span, third_span
    )
    diagonal = 6.0 + coefficient
    current = volume_field
    for repeat in range(3):
        current = relax(current, source, diagonal)
    return (current, surface_flux)


def solution(mesh):
    in_specs = (
        P(None, "row", "col", "gz"),
        P(None, "row", "col", "gz"),
        P("row", "col", "gz"),
        P("row", "col"),
        P("row", "col", "gz", None),
        P("row", "col", "gz", None),
    )
    out_specs = (P(None, "row", "col", "gz"), P("gz", ("row", "col")))
    return jax.shard_map(
        per_device, mesh=mesh, in_specs=in_specs, out_specs=out_specs, check_vma=False
    )
```

profile of v0, /device:TPU:17, one launch (start us, length us, event | category | flops | bytes accessed | tf_op | source)
XLA Modules:
  0.0 316.4 jit_solution(1257853080280869536)
XLA Ops:
  7.2 0.0 all-gather.2.cloned.1.call-start
  7.2 8.3 %fusion.22 = bf16[128,1024]{1,0:T(8,128)(2,1)} fusion(bf16[16,8,64,128]{3,2,1,0:T(8,128)(2,1)} %bitcast.27, s32[1024]{0:T(1024)} %bitcast.29), kind=kOutput, calls=%fused_computation.46 | convolution fusion | flops 2156003328 | bytes 2363392 | tf_op jit(solution)/shard_map/dot_general | solution.py:44
  15.5 0.0 all-gather.2.cloned.1.call-update
  15.5 0.0 copy-start.1
  15.6 0.0 reduce-scatter.2.cloned.1.call-start
  15.6 3.3 %copy.15 = bf16[128,8,8,128]{0,3,2,1:T(8,128)(2,1)S(1)} copy(bf16[128,8,8,128]{3,2,1,0:T(8,128)(2,1)} %param.6) | data formatting | bytes 4194304 | tf_op args[0]
  19.0 3.1 collective-permute-start
  22.1 1.3 collective-permute-start.1
  23.4 3.7 %collective-permute-done = bf16[128,1,8,128]{0,3,2,1:T(8,128)(2,1)S(1)} collective-permute-done((bf16[128,1,8,128]{0,3,2,1:T(8,128)(2,1)S(1)}, bf16[128,1,8,128]{0,3,2,1:T(8,128)(2,1)S(1)}, u32[]{:S(2)}, u32[]{:S(2)}) %collective-permute-start) | collective-permute-done | bytes 262176 | tf_op jit(solution)/shard_map/ppermute | solution.py:16
  27.1 3.8 %collective-permute-done.1 = bf16[128,1,8,128]{0,3,2,1:T(8,128)(2,1)S(1)} collective-permute-done((bf16[128,1,8,128]{0,3,2,1:T(8,128)(2,1)S(1)}, bf16[128,1,8,128]{0,3,2,1:T(8,128)(2,1)S(1)}, u32[]{:S(2)}, u32[]{:S(2)}) %collective-permute-start.1) | collective-permute-done | bytes 262176 | tf_op jit(solution)/shard_map/ppermute | solution.py:17
  30.9 0.9 pad_maximum_fusion.8
  31.8 3.5 %collective-permute-start.2 = (bf16[128,10,1,128]{0,3,2,1:T(8,128)(2,1)}, bf16[128,10,1,128]{0,3,2,1:T(8,128)(2,1)S(1)}, u32[]{:S(2)}, u32[]{:S(2)}) collective-permute-start(bf16[128,10,1,128]{0,3,2,1:T(8,128)(2,1)} %get-tuple-element.16), channel_id=1, source_target_pairs={{0,4},{4,8},{8,12},{12,16},{16,20},{20,24},{24,28},{28,32},{32,36}... | collective-permute-start | bytes 983048 | tf_op jit(solution)/shard_map/ppermute | solution.py:16
  35.4 4.5 %collective-permute-start.3 = (bf16[128,10,1,128]{0,3,2,1:T(8,128)(2,1)}, bf16[128,10,1,128]{0,3,2,1:T(8,128)(2,1)S(1)}, u32[]{:S(2)}, u32[]{:S(2)}) collective-permute-start(bf16[128,10,1,128]{0,3,2,1:T(8,128)(2,1)} %get-tuple-element.17), channel_id=1, source_target_pairs={{4,0},{8,4},{12,8},{16,12},{20,16},{24,20},{28,24},{32,28},{36,32}... | collective-permute-start | bytes 983048 | tf_op jit(solution)/shard_map/ppermute | solution.py:17
  39.9 8.5 %collective-permute-done.2 = bf16[128,10,1,128]{0,3,2,1:T(8,128)(2,1)S(1)} collective-permute-done((bf16[128,10,1,128]{0,3,2,1:T(8,128)(2,1)}, bf16[128,10,1,128]{0,3,2,1:T(8,128)(2,1)S(1)}, u32[]{:S(2)}, u32[]{:S(2)}) %collective-permute-start.2) | collective-permute-done | bytes 327712 | tf_op jit(solution)/shard_map/ppermute | solution.py:16
  48.5 5.0 %collective-permute-done.3 = bf16[128,10,1,128]{0,3,2,1:T(8,128)(2,1)S(1)} collective-permute-done((bf16[128,10,1,128]{0,3,2,1:T(8,128)(2,1)}, bf16[128,10,1,128]{0,3,2,1:T(8,128)(2,1)S(1)}, u32[]{:S(2)}, u32[]{:S(2)}) %collective-permute-start.3) | collective-permute-done | bytes 327712 | tf_op jit(solution)/shard_map/ppermute | solution.py:17
  53.5 0.1 pad_maximum_fusion.23
  53.6 8.9 %collective-permute-start.4 = (bf16[128,10,10,1]{0,3,2,1:T(2,128)(2,1)S(1)}, bf16[128,10,10,1]{0,3,2,1:T(2,128)(2,1)S(1)}, u32[]{:S(2)}, u32[]{:S(2)}) collective-permute-start(bf16[128,10,10,1]{0,3,2,1:T(2,128)(2,1)S(1)} %get-tuple-element.10), channel_id=1, source_target_pairs={{0,1},{1,2},{2,3},{4,5},{5,6},{6,7},{8,9},{9,10},{10,11},{12,13},{... | collective-permute-start | bytes 76808 | tf_op jit(solution)/shard_map/ppermute | solution.py:16
  62.5 1.9 collective-permute-start.5
  64.4 32.9 %all-gather.2.cloned.1.call-done = bf16[128,16384]{1,0:T(8,128)(2,1)} async-done(((bf16[128,1024]{1,0:T(8,128)(2,1)}), bf16[128,16384]{1,0:T(8,128)(2,1)}) %all-gather.2.cloned.1.call-update) | async-done | bytes 4194320 | tf_op jit(solution)/shard_map/all_gather | solution.py:49
  97.4 6.7 %fusion.25 = f32[32,256]{0,1:T(8,128)} fusion(bf16[256,16384]{1,0:T(8,128)(2,1)} %param.9, bf16[128,16384]{1,0:T(8,128)(2,1)} %all-gather.2.cloned.1.call-done, s32[]{:T(128)S(6)} %select_n.3), kind=kOutput, calls=%fused_computation.47 | convolution fusion | flops 268435456 | bytes 9469956 | tf_op jit(solution)/shard_map/dot_general | solution.py:54
  104.0 0.0 reduce-scatter.2.cloned.1.call-update
  104.1 4.2 %copy.16 = bf16[128,8,8,128]{0,3,2,1:T(8,128)(2,1)} copy(bf16[128,8,8,128]{3,2,1,0:T(8,128)(2,1)} %param.7) | data formatting | bytes 4194304 | tf_op args[1]
  108.3 53.4 %reduce-scatter.2.cloned.1.call-done = f32[32,16]{0,1:T(8,128)} async-done(((f32[32,256]{0,1:T(8,128)}), f32[32,16]{0,1:T(8,128)}) %reduce-scatter.2.cloned.1.call-update) | async-done | bytes 2064 | tf_op jit(solution)/shard_map/reduce_scatter | solution.py:57
  161.7 1.4 reshape.41
  163.1 17.1 %all-to-all-start = ((f32[4,1,128]{2,1,0:T(1,128)}), f32[4,1,128]{2,1,0:T(1,128)}, u32[]{:S(2)}, u32[]{:S(2)}) async-start(f32[4,1,128]{2,1,0:T(1,128)} %reshape.41), calls=%async_computation.1 | async-start | bytes 4096 | tf_op jit(solution)/shard_map/all_to_all | solution.py:58
  180.1 0.0 collective-permute-done.4
  180.1 4.7 %maximum_convert_fusion = f32[128,10,10,130]{0,3,2,1:T(8,128)} fusion(bf16[128,10,10,1]{0,3,2,1:T(2,128)(2,1)S(1)} %collective-permute-done.5, bf16[128,10,1,128]{0,3,2,1:T(8,128)(2,1)S(1)} %collective-permute-done.3, bf16[128,1,8,128]{0,3,2,1:T(8,128)(2,1)S(1)} %collective-permute-done.1, bf16[128,8,8,128]{0,3,2,1:T(8,128)(2,1)S(1)} %copy.15, ...), kind=kLoop, calls=%fused_computation.40 | loop fusion | flops 23296000 | bytes 9984000 | tf_op jit(solution)/shard_map/convert_element_type | solution.py:23
  184.9 2.0 all-to-all-done
  186.9 0.5 broadcast.32
  187.4 1.2 reduce
  188.6 0.1 reshape.42
  188.7 0.1 reshape.39
  188.8 14.0 %fusion.14 = (bf16[128,8,8,128]{0,3,2,1:T(8,128)(2,1)S(1)}, f32[128,8,8,128]{0,3,2,1:T(8,128)}) fusion(f32[128,10,10,130]{0,3,2,1:T(8,128)} %maximum_convert_fusion, bf16[128,8,8,128]{0,3,2,1:T(8,128)(2,1)S(1)} %copy.15, f32[8,8,128]{2,1,0:T(8,128)S(1)} %broadcast_add_fusion, s32[8,8,128]{2,1,0:T(8,128)S(1)} %multiply_add_fusion, s32[4]{0:T(128)S(1)} %bitcast.30, ...), kind=kOutput, calls=%fused_computation.37 | convolution fusion | flops 66093056 | bytes 35719184 | tf_op jit(solution)/shard_map/dot_general | solution.py:63
  202.8 3.0 collective-permute-start.6
  205.8 1.3 collective-permute-start.7
  207.1 3.3 %collective-permute-done.6 = bf16[128,1,8,128]{0,3,2,1:T(8,128)(2,1)S(1)} collective-permute-done((bf16[128,1,8,128]{0,3,2,1:T(8,128)(2,1)S(1)}, bf16[128,1,8,128]{0,3,2,1:T(8,128)(2,1)S(1)}, u32[]{:S(2)}, u32[]{:S(2)}) %collective-permute-start.6) | collective-permute-done | bytes 262176 | tf_op jit(solution)/shard_map/ppermute | solution.py:16
  210.4 3.8 %collective-permute-done.7 = bf16[128,1,8,128]{0,3,2,1:T(8,128)(2,1)S(1)} collective-permute-done((bf16[128,1,8,128]{0,3,2,1:T(8,128)(2,1)S(1)}, bf16[128,1,8,128]{0,3,2,1:T(8,128)(2,1)S(1)}, u32[]{:S(2)}, u32[]{:S(2)}) %collective-permute-start.7) | collective-permute-done | bytes 262176 | tf_op jit(solution)/shard_map/ppermute | solution.py:17
  214.3 0.1 pad_maximum_fusion.5
  214.4 2.8 collective-permute-start.8
  217.2 5.1 %collective-permute-start.9 = (bf16[128,10,1,128]{0,3,2,1:T(8,128)(2,1)S(1)}, bf16[128,10,1,128]{0,3,2,1:T(8,128)(2,1)S(1)}, u32[]{:S(2)}, u32[]{:S(2)}) collective-permute-start(bf16[128,10,1,128]{0,3,2,1:T(8,128)(2,1)S(1)} %get-tuple-element.15), channel_id=1, source_target_pairs={{4,0},{8,4},{12,8},{16,12},{20,16},{24,20},{28,24},{32,28},{36,32}... | collective-permute-start | bytes 983048 | tf_op jit(solution)/shard_map/ppermute | solution.py:17
  222.4 3.8 %collective-permute-done.8 = bf16[128,10,1,128]{0,3,2,1:T(8,128)(2,1)S(1)} collective-permute-done((bf16[128,10,1,128]{0,3,2,1:T(8,128)(2,1)S(1)}, bf16[128,10,1,128]{0,3,2,1:T(8,128)(2,1)S(1)}, u32[]{:S(2)}, u32[]{:S(2)}) %collective-permute-start.8) | collective-permute-done | bytes 327712 | tf_op jit(solution)/shard_map/ppermute | solution.py:16
  226.1 6.6 %collective-permute-done.9 = bf16[128,10,1,128]{0,3,2,1:T(8,128)(2,1)S(1)} collective-permute-done((bf16[128,10,1,128]{0,3,2,1:T(8,128)(2,1)S(1)}, bf16[128,10,1,128]{0,3,2,1:T(8,128)(2,1)S(1)}, u32[]{:S(2)}, u32[]{:S(2)}) %collective-permute-start.9) | collective-permute-done | bytes 327712 | tf_op jit(solution)/shard_map/ppermute | solution.py:17
  232.7 0.1 pad_maximum_fusion.18
  232.8 9.6 %collective-permute-start.10 = (bf16[128,10,10,1]{0,3,2,1:T(2,128)(2,1)S(1)}, bf16[128,10,10,1]{0,3,2,1:T(2,128)(2,1)S(1)}, u32[]{:S(2)}, u32[]{:S(2)}) collective-permute-start(bf16[128,10,10,1]{0,3,2,1:T(2,128)(2,1)S(1)} %get-tuple-element.8), channel_id=1, source_target_pairs={{0,1},{1,2},{2,3},{4,5},{5,6},{6,7},{8,9},{9,10},{10,11},{12,13},{... | collective-permute-start | bytes 76808 | tf_op jit(solution)/shard_map/ppermute | solution.py:16
  242.5 2.2 collective-permute-start.11
  244.7 7.4 %collective-permute-done.11 = bf16[128,10,10,1]{0,3,2,1:T(2,128)(2,1)S(1)} collective-permute-done((bf16[128,10,10,1]{0,3,2,1:T(2,128)(2,1)S(1)}, bf16[128,10,10,1]{0,3,2,1:T(2,128)(2,1)S(1)}, u32[]{:S(2)}, u32[]{:S(2)}) %collective-permute-start.11) | collective-permute-done | bytes 25632 | tf_op jit(solution)/shard_map/ppermute | solution.py:17
  252.1 3.0 maximum_convert_fusion.1
  255.1 4.5 %fusion.15 = bf16[128,8,8,128]{0,3,2,1:T(8,128)(2,1)S(1)} fusion(f32[128,8,8,128]{0,3,2,1:T(8,128)S(1)} %copy-done, f32[128,10,10,130]{0,3,2,1:T(8,128)S(1)} %maximum_convert_fusion.1, bf16[128,8,8,128]{0,3,2,1:T(8,128)(2,1)S(1)} %get-tuple-element.24, f32[8,8,128]{2,1,0:T(8,128)S(1)} %broadcast_add_fusion), kind=kLoop, calls=%fused_computation.38 | loop fusion | flops 13631488 | bytes 33587200 | tf_op jit(solution)/shard_map/convert_element_type | solution.py:28
  259.7 3.1 collective-permute-start.12
  262.8 1.3 collective-permute-start.13
  264.1 2.0 collective-permute-done.12
  266.0 3.8 %collective-permute-done.13 = bf16[128,1,8,128]{0,3,2,1:T(8,128)(2,1)S(1)} collective-permute-done((bf16[128,1,8,128]{0,3,2,1:T(8,128)(2,1)S(1)}, bf16[128,1,8,128]{0,3,2,1:T(8,128)(2,1)S(1)}, u32[]{:S(2)}, u32[]{:S(2)}) %collective-permute-start.13) | collective-permute-done | bytes 262176 | tf_op jit(solution)/shard_map/ppermute | solution.py:17
  269.9 0.1 pad_maximum_fusion.2
  270.0 4.6 %collective-permute-start.14 = (bf16[128,10,1,128]{0,3,2,1:T(8,128)(2,1)S(1)}, bf16[128,10,1,128]{0,3,2,1:T(8,128)(2,1)S(1)}, u32[]{:S(2)}, u32[]{:S(2)}) collective-permute-start(bf16[128,10,1,128]{0,3,2,1:T(8,128)(2,1)S(1)} %get-tuple-element.12), channel_id=1, source_target_pairs={{0,4},{4,8},{8,12},{12,16},{16,20},{20,24},{24,28},{28,32},{32,36}... | collective-permute-start | bytes 983048 | tf_op jit(solution)/shard_map/ppermute | solution.py:16
  274.5 3.4 %collective-permute-start.15 = (bf16[128,10,1,128]{0,3,2,1:T(8,128)(2,1)S(1)}, bf16[128,10,1,128]{0,3,2,1:T(8,128)(2,1)S(1)}, u32[]{:S(2)}, u32[]{:S(2)}) collective-permute-start(bf16[128,10,1,128]{0,3,2,1:T(8,128)(2,1)S(1)} %get-tuple-element.13), channel_id=1, source_target_pairs={{4,0},{8,4},{12,8},{16,12},{20,16},{24,20},{28,24},{32,28},{36,32}... | collective-permute-start | bytes 983048 | tf_op jit(solution)/shard_map/ppermute | solution.py:17
  278.0 5.4 %collective-permute-done.14 = bf16[128,10,1,128]{0,3,2,1:T(8,128)(2,1)S(1)} collective-permute-done((bf16[128,10,1,128]{0,3,2,1:T(8,128)(2,1)S(1)}, bf16[128,10,1,128]{0,3,2,1:T(8,128)(2,1)S(1)}, u32[]{:S(2)}, u32[]{:S(2)}) %collective-permute-start.14) | collective-permute-done | bytes 327712 | tf_op jit(solution)/shard_map/ppermute | solution.py:16
  283.3 4.6 %collective-permute-done.15 = bf16[128,10,1,128]{0,3,2,1:T(8,128)(2,1)S(1)} collective-permute-done((bf16[128,10,1,128]{0,3,2,1:T(8,128)(2,1)S(1)}, bf16[128,10,1,128]{0,3,2,1:T(8,128)(2,1)S(1)}, u32[]{:S(2)}, u32[]{:S(2)}) %collective-permute-start.15) | collective-permute-done | bytes 327712 | tf_op jit(solution)/shard_map/ppermute | solution.py:17
  287.9 0.1 pad_maximum_fusion.13
  288.0 1.9 collective-permute-start.16
  289.9 2.4 collective-permute-start.17
  292.3 6.9 %collective-permute-done.17 = bf16[128,10,10,1]{0,3,2,1:T(2,128)(2,1)S(1)} collective-permute-done((bf16[128,10,10,1]{0,3,2,1:T(2,128)(2,1)S(1)}, bf16[128,10,10,1]{0,3,2,1:T(2,128)(2,1)S(1)}, u32[]{:S(2)}, u32[]{:S(2)}) %collective-permute-start.17) | collective-permute-done | bytes 25632 | tf_op jit(solution)/shard_map/ppermute | solution.py:17
  299.3 3.0 maximum_convert_fusion.2
  302.2 4.5 %fusion.16 = bf16[128,8,8,128]{0,3,2,1:T(8,128)(2,1)S(1)} fusion(f32[128,8,8,128]{0,3,2,1:T(8,128)S(1)} %copy-done, f32[128,10,10,130]{0,3,2,1:T(8,128)S(1)} %maximum_convert_fusion.2, bf16[128,8,8,128]{0,3,2,1:T(8,128)(2,1)S(1)} %fusion.15, f32[8,8,128]{2,1,0:T(8,128)S(1)} %broadcast_add_fusion), kind=kLoop, calls=%fused_computation.39 | loop fusion | flops 13631488 | bytes 33587200 | tf_op jit(solution)/shard_map/convert_element_type | solution.py:28
  306.8 2.8 copy.21
  (15 shorter events, 0.2 us)
Async XLA Ops:
  7.2 90.2 %all-gather.2.cloned.1.call-start = ((), (), s32[]{:S(2)}) async-start(), calls=%async_computation.2 | async-start | bytes 4456448 | tf_op jit(solution)/shard_map/all_gather | solution.py:49
  15.5 24.4 %copy-start.1 = (f32[8,8,128]{2,1,0:T(8,128)S(1)}, f32[8,8,128]{2,1,0:T(8,128)}, u32[]{:S(2)}) copy-start(f32[8,8,128]{2,1,0:T(8,128)} %param.8) | copy-start | bytes 98308
  15.6 146.1 %reduce-scatter.2.cloned.1.call-start = ((), (), s32[]{:S(2)}) async-start(), calls=%async_computation.3 | async-start | bytes 139264 | tf_op jit(solution)/shard_map/reduce_scatter | solution.py:57
  19.0 8.1 %collective-permute-start = (bf16[128,1,8,128]{0,3,2,1:T(8,128)(2,1)S(1)}, bf16[128,1,8,128]{0,3,2,1:T(8,128)(2,1)S(1)}, u32[]{:S(2)}, u32[]{:S(2)}) collective-permute-start(bf16[128,1,8,128]{0,3,2,1:T(8,128)(2,1)S(1)} %get-tuple-element.22), channel_id=1, source_target_pairs={{0,64},{64,128},{128,192},{1,65},{65,129},{129,193},{2,66},{66,130... | collective-permute-start | bytes 786440 | tf_op jit(solution)/shard_map/ppermute | solution.py:16
  22.1 8.8 %collective-permute-start.1 = (bf16[128,1,8,128]{0,3,2,1:T(8,128)(2,1)S(1)}, bf16[128,1,8,128]{0,3,2,1:T(8,128)(2,1)S(1)}, u32[]{:S(2)}, u32[]{:S(2)}) collective-permute-start(bf16[128,1,8,128]{0,3,2,1:T(8,128)(2,1)S(1)} %get-tuple-element.23), channel_id=1, source_target_pairs={{64,0},{128,64},{192,128},{65,1},{129,65},{193,129},{66,2},{130,66... | collective-permute-start | bytes 786440 | tf_op jit(solution)/shard_map/ppermute | solution.py:17
  31.8 16.6 %collective-permute-start.2 = (bf16[128,10,1,128]{0,3,2,1:T(8,128)(2,1)}, bf16[128,10,1,128]{0,3,2,1:T(8,128)(2,1)S(1)}, u32[]{:S(2)}, u32[]{:S(2)}) collective-permute-start(bf16[128,10,1,128]{0,3,2,1:T(8,128)(2,1)} %get-tuple-element.16), channel_id=1, source_target_pairs={{0,4},{4,8},{8,12},{12,16},{16,20},{20,24},{24,28},{28,32},{32,36}... | collective-permute-start | bytes 983048 | tf_op jit(solution)/shard_map/ppermute | solution.py:16
  35.4 18.1 %collective-permute-start.3 = (bf16[128,10,1,128]{0,3,2,1:T(8,128)(2,1)}, bf16[128,10,1,128]{0,3,2,1:T(8,128)(2,1)S(1)}, u32[]{:S(2)}, u32[]{:S(2)}) collective-permute-start(bf16[128,10,1,128]{0,3,2,1:T(8,128)(2,1)} %get-tuple-element.17), channel_id=1, source_target_pairs={{4,0},{8,4},{12,8},{16,12},{20,16},{24,20},{28,24},{32,28},{36,32}... | collective-permute-start | bytes 983048 | tf_op jit(solution)/shard_map/ppermute | solution.py:17
  53.6 126.6 %collective-permute-start.4 = (bf16[128,10,10,1]{0,3,2,1:T(2,128)(2,1)S(1)}, bf16[128,10,10,1]{0,3,2,1:T(2,128)(2,1)S(1)}, u32[]{:S(2)}, u32[]{:S(2)}) collective-permute-start(bf16[128,10,10,1]{0,3,2,1:T(2,128)(2,1)S(1)} %get-tuple-element.10), channel_id=1, source_target_pairs={{0,1},{1,2},{2,3},{4,5},{5,6},{6,7},{8,9},{9,10},{10,11},{12,13},{... | collective-permute-start | bytes 76808 | tf_op jit(solution)/shard_map/ppermute | solution.py:16
  62.5 117.6 %collective-permute-start.5 = (bf16[128,10,10,1]{0,3,2,1:T(2,128)(2,1)S(1)}, bf16[128,10,10,1]{0,3,2,1:T(2,128)(2,1)S(1)}, u32[]{:S(2)}, u32[]{:S(2)}) collective-permute-start(bf16[128,10,10,1]{0,3,2,1:T(2,128)(2,1)S(1)} %get-tuple-element.11), channel_id=1, source_target_pairs={{1,0},{2,1},{3,2},{5,4},{6,5},{7,6},{9,8},{10,9},{11,10},{13,12},{... | collective-permute-start | bytes 76808 | tf_op jit(solution)/shard_map/ppermute | solution.py:17
  163.1 23.9 %all-to-all-start = ((f32[4,1,128]{2,1,0:T(1,128)}), f32[4,1,128]{2,1,0:T(1,128)}, u32[]{:S(2)}, u32[]{:S(2)}) async-start(f32[4,1,128]{2,1,0:T(1,128)} %reshape.41), calls=%async_computation.1 | async-start | bytes 4096 | tf_op jit(solution)/shard_map/all_to_all | solution.py:58
  180.1 8.7 %copy-start.2 = (s32[1,1,1,4]{3,2,1,0:T(1,128)S(1)}, s32[1,1,1,4]{3,2,1,0:T(1,128)}, u32[]{:S(2)}) copy-start(s32[1,1,1,4]{3,2,1,0:T(1,128)} %param.11) | copy-start | bytes 52
  202.8 7.6 %collective-permute-start.6 = (bf16[128,1,8,128]{0,3,2,1:T(8,128)(2,1)S(1)}, bf16[128,1,8,128]{0,3,2,1:T(8,128)(2,1)S(1)}, u32[]{:S(2)}, u32[]{:S(2)}) collective-permute-start(bf16[128,1,8,128]{0,3,2,1:T(8,128)(2,1)S(1)} %get-tuple-element.20), channel_id=1, source_target_pairs={{0,64},{64,128},{128,192},{1,65},{65,129},{129,193},{2,66},{66,130... | collective-permute-start | bytes 786440 | tf_op jit(solution)/shard_map/ppermute | solution.py:16
  205.8 8.5 %collective-permute-start.7 = (bf16[128,1,8,128]{0,3,2,1:T(8,128)(2,1)S(1)}, bf16[128,1,8,128]{0,3,2,1:T(8,128)(2,1)S(1)}, u32[]{:S(2)}, u32[]{:S(2)}) collective-permute-start(bf16[128,1,8,128]{0,3,2,1:T(8,128)(2,1)S(1)} %get-tuple-element.21), channel_id=1, source_target_pairs={{64,0},{128,64},{192,128},{65,1},{129,65},{193,129},{66,2},{130,66... | collective-permute-start | bytes 786440 | tf_op jit(solution)/shard_map/ppermute | solution.py:17
  214.4 11.8 %collective-permute-start.8 = (bf16[128,10,1,128]{0,3,2,1:T(8,128)(2,1)S(1)}, bf16[128,10,1,128]{0,3,2,1:T(8,128)(2,1)S(1)}, u32[]{:S(2)}, u32[]{:S(2)}) collective-permute-start(bf16[128,10,1,128]{0,3,2,1:T(8,128)(2,1)S(1)} %get-tuple-element.14), channel_id=1, source_target_pairs={{0,4},{4,8},{8,12},{12,16},{16,20},{20,24},{24,28},{28,32},{32,36}... | collective-permute-start | bytes 983048 | tf_op jit(solution)/shard_map/ppermute | solution.py:16
  217.2 15.5 %collective-permute-start.9 = (bf16[128,10,1,128]{0,3,2,1:T(8,128)(2,1)S(1)}, bf16[128,10,1,128]{0,3,2,1:T(8,128)(2,1)S(1)}, u32[]{:S(2)}, u32[]{:S(2)}) collective-permute-start(bf16[128,10,1,128]{0,3,2,1:T(8,128)(2,1)S(1)} %get-tuple-element.15), channel_id=1, source_target_pairs={{4,0},{8,4},{12,8},{16,12},{20,16},{24,20},{28,24},{32,28},{36,32}... | collective-permute-start | bytes 983048 | tf_op jit(solution)/shard_map/ppermute | solution.py:17
  232.8 11.9 %collective-permute-start.10 = (bf16[128,10,10,1]{0,3,2,1:T(2,128)(2,1)S(1)}, bf16[128,10,10,1]{0,3,2,1:T(2,128)(2,1)S(1)}, u32[]{:S(2)}, u32[]{:S(2)}) collective-permute-start(bf16[128,10,10,1]{0,3,2,1:T(2,128)(2,1)S(1)} %get-tuple-element.8), channel_id=1, source_target_pairs={{0,1},{1,2},{2,3},{4,5},{5,6},{6,7},{8,9},{9,10},{10,11},{12,13},{... | collective-permute-start | bytes 76808 | tf_op jit(solution)/shard_map/ppermute | solution.py:16
  242.5 12.6 %copy-start = (f32[128,8,8,128]{0,3,2,1:T(8,128)S(1)}, f32[128,8,8,128]{0,3,2,1:T(8,128)}, u32[]{:S(2)}) copy-start(f32[128,8,8,128]{0,3,2,1:T(8,128)} %get-tuple-element.25) | copy-start | bytes 12582916
  242.5 9.6 %collective-permute-start.11 = (bf16[128,10,10,1]{0,3,2,1:T(2,128)(2,1)S(1)}, bf16[128,10,10,1]{0,3,2,1:T(2,128)(2,1)S(1)}, u32[]{:S(2)}, u32[]{:S(2)}) collective-permute-start(bf16[128,10,10,1]{0,3,2,1:T(2,128)(2,1)S(1)} %get-tuple-element.9), channel_id=1, source_target_pairs={{1,0},{2,1},{3,2},{5,4},{6,5},{7,6},{9,8},{10,9},{11,10},{13,12},{... | collective-permute-start | bytes 76808 | tf_op jit(solution)/shard_map/ppermute | solution.py:17
  259.7 6.4 %collective-permute-start.12 = (bf16[128,1,8,128]{0,3,2,1:T(8,128)(2,1)S(1)}, bf16[128,1,8,128]{0,3,2,1:T(8,128)(2,1)S(1)}, u32[]{:S(2)}, u32[]{:S(2)}) collective-permute-start(bf16[128,1,8,128]{0,3,2,1:T(8,128)(2,1)S(1)} %get-tuple-element.18), channel_id=1, source_target_pairs={{0,64},{64,128},{128,192},{1,65},{65,129},{129,193},{2,66},{66,130... | collective-permute-start | bytes 786440 | tf_op jit(solution)/shard_map/ppermute | solution.py:16
  262.8 7.1 %collective-permute-start.13 = (bf16[128,1,8,128]{0,3,2,1:T(8,128)(2,1)S(1)}, bf16[128,1,8,128]{0,3,2,1:T(8,128)(2,1)S(1)}, u32[]{:S(2)}, u32[]{:S(2)}) collective-permute-start(bf16[128,1,8,128]{0,3,2,1:T(8,128)(2,1)S(1)} %get-tuple-element.19), channel_id=1, source_target_pairs={{64,0},{128,64},{192,128},{65,1},{129,65},{193,129},{66,2},{130,66... | collective-permute-start | bytes 786440 | tf_op jit(solution)/shard_map/ppermute | solution.py:17
  270.0 13.4 %collective-permute-start.14 = (bf16[128,10,1,128]{0,3,2,1:T(8,128)(2,1)S(1)}, bf16[128,10,1,128]{0,3,2,1:T(8,128)(2,1)S(1)}, u32[]{:S(2)}, u32[]{:S(2)}) collective-permute-start(bf16[128,10,1,128]{0,3,2,1:T(8,128)(2,1)S(1)} %get-tuple-element.12), channel_id=1, source_target_pairs={{0,4},{4,8},{8,12},{12,16},{16,20},{20,24},{24,28},{28,32},{32,36}... | collective-permute-start | bytes 983048 | tf_op jit(solution)/shard_map/ppermute | solution.py:16
  274.5 13.4 %collective-permute-start.15 = (bf16[128,10,1,128]{0,3,2,1:T(8,128)(2,1)S(1)}, bf16[128,10,1,128]{0,3,2,1:T(8,128)(2,1)S(1)}, u32[]{:S(2)}, u32[]{:S(2)}) collective-permute-start(bf16[128,10,1,128]{0,3,2,1:T(8,128)(2,1)S(1)} %get-tuple-element.13), channel_id=1, source_target_pairs={{4,0},{8,4},{12,8},{16,12},{20,16},{24,20},{28,24},{32,28},{36,32}... | collective-permute-start | bytes 983048 | tf_op jit(solution)/shard_map/ppermute | solution.py:17
  288.0 4.3 %collective-permute-start.16 = (bf16[128,10,10,1]{0,3,2,1:T(2,128)(2,1)S(1)}, bf16[128,10,10,1]{0,3,2,1:T(2,128)(2,1)S(1)}, u32[]{:S(2)}, u32[]{:S(2)}) collective-permute-start(bf16[128,10,10,1]{0,3,2,1:T(2,128)(2,1)S(1)} %get-tuple-element.6), channel_id=1, source_target_pairs={{0,1},{1,2},{2,3},{4,5},{5,6},{6,7},{8,9},{9,10},{10,11},{12,13},{... | collective-permute-start | bytes 76808 | tf_op jit(solution)/shard_map/ppermute | solution.py:16
  289.9 9.3 %collective-permute-start.17 = (bf16[128,10,10,1]{0,3,2,1:T(2,128)(2,1)S(1)}, bf16[128,10,10,1]{0,3,2,1:T(2,128)(2,1)S(1)}, u32[]{:S(2)}, u32[]{:S(2)}) collective-permute-start(bf16[128,10,10,1]{0,3,2,1:T(2,128)(2,1)S(1)} %get-tuple-element.7), channel_id=1, source_target_pairs={{1,0},{2,1},{3,2},{5,4},{6,5},{7,6},{9,8},{10,9},{11,10},{13,12},{... | collective-permute-start | bytes 76808 | tf_op jit(solution)/shard_map/ppermute | solution.py:17
Sparse Core Ops, SparseCore 0:
  15.7 81.6 all-gather.1
  104.2 57.4 reduce-scatter.1
where the time goes:
time: 317 us; the launch traced here: 316 us
  waiting for transfers between devices  157 us (50%)
  starting transfers between devices  81.2 us (26%)
  matrix products  28.9 us (9%)
  other arithmetic  22.3 us (7%)
  between operations  14.3 us (5%)
  local copies, waits for them, and re-layouts  12.4 us (4%)
    reduce_scatter x1, waiting for transfers between devices, per_device(): lax.psum_scatter(partial_flux, 'col', scatter_dimension=1, tiled=True)  53.4 us
    ppermute x9, waiting for transfers between devices, padded_2(): after = lax.ppermute(first, axis, down)  42 us
    ppermute x9, starting transfers between devices, padded_2(): before = lax.ppermute(last, axis, up)  40.6 us
    all_gather x1, waiting for transfers between devices, per_device(): lax.all_gather(trace_values, ('row', 'gz'), axis=1, tiled=True)  32.9 us
    ppermute x9, waiting for transfers between devices, padded_2(): before = lax.ppermute(last, axis, up)  26.7 us
    ppermute x9, starting transfers between devices, padded_2(): after = lax.ppermute(first, axis, down)  23.4 us
    all_to_all x1, starting transfers between devices, per_device(): lax.all_to_all(surface_flux, 'gz', split_axis=1, concat_axis=0, tiled=True)  17.1 us
    dot_general x1, matrix products, per_device(): jnp.dot(owned_flux, placer, precision=lax.Precision.HIGHEST, preferred_el...  14 us
  transfers between devices with their start and end apart: 21, of which 17 were waited for; matrix products, arithmetic and copies ran while one was open for 7% of the time, Pallas kernels for 0%

commit v1 on v0

--- a/solution.py
+++ b/solution.py
@@ -1,9 +1,23 @@
+import functools
 import jax
 import jax.numpy as jnp
 from jax import lax
 from jax.sharding import PartitionSpec as P
 
 OMEGA = 0.8
+
+
+def link_case_up(field, at_axis):
+    ledger = []
+    for _ in range(lax.axis_size(("row", "gz"))):
+        ledger.append(field)
+    return jnp.concatenate(
+        lax.all_to_all(jnp.stack(ledger), axis_name=("row", "gz"), split_axis=0, concat_axis=0),
+        axis=at_axis,
+    )
+
+
+manage_columns_up = functools.partial(link_case_up, at_axis=1)
 
 
 def padded_2(array, sides, width):
@@ -46,10 +60,7 @@
     )
     layer_index = lax.axis_index("gz")
     chosen = lax.dynamic_slice_in_dim(
-        lax.all_gather(trace_values, ("row", "gz"), axis=1, tiled=True),
-        layer_index * side_group,
-        side_group,
-        0,
+        manage_columns_up(trace_values), layer_index * side_group, side_group, 0
     )
     partial_flux = lax.dot_general(
         chosen, surface_block, (((1,), (1,)), ((), ())), preferred_element_type=jnp.float32

time: 317 us -> 371 us (1.17)
  waiting for transfers between devices: 157 us -> 202 us
  starting transfers between devices: 81.2 us -> 88.1 us
    ppermute x9, waiting for transfers between devices: 26.7 us -> 90.9 us  [padded_2(): before = lax.ppermute(last, axis, up)]
    all_gather x1 -> x0, waiting for transfers between devices: 32.9 us -> none  [per_device(): lax.all_gather(trace_values, ('row', 'gz'), axis=1, tiled=True)]
    all_to_all x0 -> x1, starting transfers between devices: none -> 11.6 us  [link_case_up(): lax.all_to_all(jnp.stack(ledger), axis_name=('row', 'gz'), split_axis=0,...]
    ppermute x9, waiting for transfers between devices: 42 us -> 49.1 us  [padded_2(): after = lax.ppermute(first, axis, down)]
    ppermute x9, starting transfers between devices: 40.6 us -> 34.3 us  [padded_2(): before = lax.ppermute(last, axis, up)]
    reduce_scatter x1, waiting for transfers between devices: 53.4 us -> 59.1 us  [per_device(): lax.psum_scatter(partial_flux, 'col', scatter_dimension=1, tiled=True)]
  transfers between devices with their start and end apart: 21 -> 21, of which waited for: 17 -> 16; matrix products, arithmetic and copies ran while one was open for 7% -> 6% of each run, Pallas kernels for 0% -> 0%
where the time goes in v1:
time: 371 us; the launch traced here: 370 us
  waiting for transfers between devices  202 us (54%)
  starting transfers between devices  88.1 us (24%)
  matrix products  28.1 us (8%)
  other arithmetic  22.4 us (6%)
  local copies, waits for them, and re-layouts  15.3 us (4%)
  between operations  14.3 us (4%)
    ppermute x9, waiting for transfers between devices, padded_2(): before = lax.ppermute(last, axis, up)  90.9 us
    reduce_scatter x1, waiting for transfers between devices, per_device(): lax.psum_scatter(partial_flux, 'col', scatter_dimension=1, tiled=True)  59.1 us
    ppermute x9, waiting for transfers between devices, padded_2(): after = lax.ppermute(first, axis, down)  49.1 us
    ppermute x9, starting transfers between devices, padded_2(): before = lax.ppermute(last, axis, up)  34.3 us
    ppermute x9, starting transfers between devices, padded_2(): after = lax.ppermute(first, axis, down)  25.1 us
    all_to_all x1, starting transfers between devices, per_device(): lax.all_to_all(surface_flux, 'gz', split_axis=1, concat_axis=0, tiled=True)  17.1 us
    dot_general x1, matrix products, per_device(): jnp.dot(owned_flux, placer, precision=lax.Precision.HIGHEST, preferred_el...  14 us
    unnamed x11, local copies, waits for them, and re-layouts  11.7 us
  transfers between devices with their start and end apart: 21, of which 16 were waited for; matrix products, arithmetic and copies ran while one was open for 6% of the time, Pallas kernels for 0%

profile of v1, /device:TPU:17, one launch (start us, length us, event | category | flops | bytes accessed | tf_op | source)
XLA Modules:
  0.0 369.8 jit_solution(977284615711343569)
XLA Ops:
  7.2 6.3 %fusion.28 = bf16[128,1024]{0,1:T(8,128)(2,1)S(1)} fusion(bf16[16,8,64,128]{3,2,1,0:T(8,128)(2,1)} %bitcast.30, s32[1024]{0:T(1024)} %bitcast.32), kind=kOutput, calls=%fused_computation.49 | convolution fusion | flops 2164391936 | bytes 2363392 | tf_op jit(solution)/shard_map/dot_general | solution.py:58
  13.5 2.8 stack.2
  16.3 11.6 %all-to-all-start = ((bf16[16,128,1024]{1,2,0:T(8,128)(2,1)}), bf16[16,128,1024]{1,2,0:T(8,128)(2,1)}, u32[]{:S(2)}, u32[]{:S(2)}) async-start(bf16[16,128,1024]{1,2,0:T(8,128)(2,1)} %stack.2), calls=%async_computation | async-start | bytes 8388608 | tf_op jit(solution)/shard_map/all_to_all | solution.py:15
  27.9 0.0 reduce-scatter.2.cloned.1.call-start
  28.0 3.3 copy.16
  31.4 3.3 collective-permute-start
  34.6 1.3 collective-permute-start.1
  35.9 39.0 %collective-permute-done = bf16[128,1,8,128]{0,3,2,1:T(8,128)(2,1)S(1)} collective-permute-done((bf16[128,1,8,128]{0,3,2,1:T(8,128)(2,1)S(1)}, bf16[128,1,8,128]{0,3,2,1:T(8,128)(2,1)S(1)}, u32[]{:S(2)}, u32[]{:S(2)}) %collective-permute-start) | collective-permute-done | bytes 262176 | tf_op jit(solution)/shard_map/ppermute | solution.py:30
  74.9 6.0 %collective-permute-done.1 = bf16[128,1,8,128]{0,3,2,1:T(8,128)(2,1)S(1)} collective-permute-done((bf16[128,1,8,128]{0,3,2,1:T(8,128)(2,1)S(1)}, bf16[128,1,8,128]{0,3,2,1:T(8,128)(2,1)S(1)}, u32[]{:S(2)}, u32[]{:S(2)}) %collective-permute-start.1) | collective-permute-done | bytes 262176 | tf_op jit(solution)/shard_map/ppermute | solution.py:31
  80.9 1.0 pad_maximum_fusion.8
  81.9 1.9 collective-permute-start.2
  83.8 6.1 %collective-permute-start.3 = (bf16[128,10,1,128]{0,3,2,1:T(8,128)(2,1)}, bf16[128,10,1,128]{0,3,2,1:T(8,128)(2,1)S(1)}, u32[]{:S(2)}, u32[]{:S(2)}) collective-permute-start(bf16[128,10,1,128]{0,3,2,1:T(8,128)(2,1)} %get-tuple-element.17), channel_id=1, source_target_pairs={{4,0},{8,4},{12,8},{16,12},{20,16},{24,20},{28,24},{32,28},{36,32}... | collective-permute-start | bytes 983048 | tf_op jit(solution)/shard_map/ppermute | solution.py:31
  89.9 36.6 %collective-permute-done.2 = bf16[128,10,1,128]{0,3,2,1:T(8,128)(2,1)S(1)} collective-permute-done((bf16[128,10,1,128]{0,3,2,1:T(8,128)(2,1)}, bf16[128,10,1,128]{0,3,2,1:T(8,128)(2,1)S(1)}, u32[]{:S(2)}, u32[]{:S(2)}) %collective-permute-start.2) | collective-permute-done | bytes 327712 | tf_op jit(solution)/shard_map/ppermute | solution.py:30
  126.5 9.2 %collective-permute-done.3 = bf16[128,10,1,128]{0,3,2,1:T(8,128)(2,1)S(1)} collective-permute-done((bf16[128,10,1,128]{0,3,2,1:T(8,128)(2,1)}, bf16[128,10,1,128]{0,3,2,1:T(8,128)(2,1)S(1)}, u32[]{:S(2)}, u32[]{:S(2)}) %collective-permute-start.3) | collective-permute-done | bytes 327712 | tf_op jit(solution)/shard_map/ppermute | solution.py:31
  135.7 0.1 pad_maximum_fusion.23
  135.7 6.1 %collective-permute-start.4 = (bf16[128,10,10,1]{0,3,2,1:T(2,128)(2,1)S(1)}, bf16[128,10,10,1]{0,3,2,1:T(2,128)(2,1)S(1)}, u32[]{:S(2)}, u32[]{:S(2)}) collective-permute-start(bf16[128,10,10,1]{0,3,2,1:T(2,128)(2,1)S(1)} %get-tuple-element.10), channel_id=1, source_target_pairs={{0,1},{1,2},{2,3},{4,5},{5,6},{6,7},{8,9},{9,10},{10,11},{12,13},{... | collective-permute-start | bytes 76808 | tf_op jit(solution)/shard_map/ppermute | solution.py:30
  141.9 1.9 collective-permute-start.5
  143.8 0.0 all-to-all-done
  143.8 7.7 %fusion.16 = f32[32,256]{0,1:T(8,128)} fusion(bf16[256,16384]{1,0:T(8,128)(2,1)} %param.9, bf16[128,16384]{0,1:T(8,128)(2,1)} %bitcast.3, s32[]{:T(128)S(6)} %select_n.3), kind=kOutput, calls=%fused_computation.37 | convolution fusion | flops 268435456 | bytes 12615684 | tf_op jit(solution)/shard_map/dot_general | solution.py:65
  151.6 0.0 reduce-scatter.2.cloned.1.call-update
  151.6 4.2 %copy.17 = bf16[128,8,8,128]{0,3,2,1:T(8,128)(2,1)} copy(bf16[128,8,8,128]{3,2,1,0:T(8,128)(2,1)} %param.7) | data formatting | bytes 4194304 | tf_op args[1]
  155.8 59.1 %reduce-scatter.2.cloned.1.call-done = f32[32,16]{0,1:T(8,128)} async-done(((f32[32,256]{0,1:T(8,128)}), f32[32,16]{0,1:T(8,128)}) %reduce-scatter.2.cloned.1.call-update) | async-done | bytes 2064 | tf_op jit(solution)/shard_map/reduce_scatter | solution.py:68
  214.9 1.4 reshape.51
  216.3 17.1 %all-to-all-start.1 = ((f32[4,1,128]{2,1,0:T(1,128)}), f32[4,1,128]{2,1,0:T(1,128)}, u32[]{:S(2)}, u32[]{:S(2)}) async-start(f32[4,1,128]{2,1,0:T(1,128)} %reshape.51), calls=%async_computation.2 | async-start | bytes 4096 | tf_op jit(solution)/shard_map/all_to_all | solution.py:69
  233.4 0.0 collective-permute-done.4
  233.4 0.0 collective-permute-done.5
  233.4 4.7 %maximum_convert_fusion = f32[128,10,10,130]{0,3,2,1:T(8,128)} fusion(bf16[128,10,10,1]{0,3,2,1:T(2,128)(2,1)S(1)} %collective-permute-done.5, bf16[128,10,1,128]{0,3,2,1:T(8,128)(2,1)S(1)} %collective-permute-done.3, bf16[128,1,8,128]{0,3,2,1:T(8,128)(2,1)S(1)} %collective-permute-done.1, bf16[128,8,8,128]{0,3,2,1:T(8,128)(2,1)S(1)} %copy.16, ...), kind=kLoop, calls=%fused_computation.43 | loop fusion | flops 23296000 | bytes 9984000 | tf_op jit(solution)/shard_map/convert_element_type | solution.py:37
  238.1 2.3 all-to-all-done.1
  240.5 0.5 broadcast.34
  241.0 1.3 reduce
  242.3 0.1 reshape.52
  242.4 0.1 reshape.49
  242.5 14.0 %fusion.18 = (bf16[128,8,8,128]{0,3,2,1:T(8,128)(2,1)S(1)}, f32[128,8,8,128]{0,3,2,1:T(8,128)}) fusion(f32[128,10,10,130]{0,3,2,1:T(8,128)} %maximum_convert_fusion, bf16[128,8,8,128]{0,3,2,1:T(8,128)(2,1)S(1)} %copy.16, f32[8,8,128]{2,1,0:T(8,128)S(1)} %broadcast_add_fusion, s32[8,8,128]{2,1,0:T(8,128)S(1)} %multiply_add_fusion, s32[4]{0:T(128)S(1)} %bitcast.33, ...), kind=kOutput, calls=%fused_computation.40 | convolution fusion | flops 66093056 | bytes 35719184 | tf_op jit(solution)/shard_map/dot_general | solution.py:74
  256.6 3.1 collective-permute-start.6
  259.7 1.3 collective-permute-start.7
  261.0 3.8 %collective-permute-done.6 = bf16[128,1,8,128]{0,3,2,1:T(8,128)(2,1)S(1)} collective-permute-done((bf16[128,1,8,128]{0,3,2,1:T(8,128)(2,1)S(1)}, bf16[128,1,8,128]{0,3,2,1:T(8,128)(2,1)S(1)}, u32[]{:S(2)}, u32[]{:S(2)}) %collective-permute-start.6) | collective-permute-done | bytes 262176 | tf_op jit(solution)/shard_map/ppermute | solution.py:30
  264.8 3.8 %collective-permute-done.7 = bf16[128,1,8,128]{0,3,2,1:T(8,128)(2,1)S(1)} collective-permute-done((bf16[128,1,8,128]{0,3,2,1:T(8,128)(2,1)S(1)}, bf16[128,1,8,128]{0,3,2,1:T(8,128)(2,1)S(1)}, u32[]{:S(2)}, u32[]{:S(2)}) %collective-permute-start.7) | collective-permute-done | bytes 262176 | tf_op jit(solution)/shard_map/ppermute | solution.py:31
  268.6 0.1 pad_maximum_fusion.5
  268.7 2.8 collective-permute-start.8
  271.6 5.2 %collective-permute-start.9 = (bf16[128,10,1,128]{0,3,2,1:T(8,128)(2,1)S(1)}, bf16[128,10,1,128]{0,3,2,1:T(8,128)(2,1)S(1)}, u32[]{:S(2)}, u32[]{:S(2)}) collective-permute-start(bf16[128,10,1,128]{0,3,2,1:T(8,128)(2,1)S(1)} %get-tuple-element.15), channel_id=1, source_target_pairs={{4,0},{8,4},{12,8},{16,12},{20,16},{24,20},{28,24},{32,28},{36,32}... | collective-permute-start | bytes 983048 | tf_op jit(solution)/shard_map/ppermute | solution.py:31
  276.7 4.2 %collective-permute-done.8 = bf16[128,10,1,128]{0,3,2,1:T(8,128)(2,1)S(1)} collective-permute-done((bf16[128,10,1,128]{0,3,2,1:T(8,128)(2,1)S(1)}, bf16[128,10,1,128]{0,3,2,1:T(8,128)(2,1)S(1)}, u32[]{:S(2)}, u32[]{:S(2)}) %collective-permute-start.8) | collective-permute-done | bytes 327712 | tf_op jit(solution)/shard_map/ppermute | solution.py:30
  281.0 7.4 %collective-permute-done.9 = bf16[128,10,1,128]{0,3,2,1:T(8,128)(2,1)S(1)} collective-permute-done((bf16[128,10,1,128]{0,3,2,1:T(8,128)(2,1)S(1)}, bf16[128,10,1,128]{0,3,2,1:T(8,128)(2,1)S(1)}, u32[]{:S(2)}, u32[]{:S(2)}) %collective-permute-start.9) | collective-permute-done | bytes 327712 | tf_op jit(solution)/shard_map/ppermute | solution.py:31
  288.3 0.1 pad_maximum_fusion.18
  288.4 7.5 %collective-permute-start.10 = (bf16[128,10,10,1]{0,3,2,1:T(2,128)(2,1)S(1)}, bf16[128,10,10,1]{0,3,2,1:T(2,128)(2,1)S(1)}, u32[]{:S(2)}, u32[]{:S(2)}) collective-permute-start(bf16[128,10,10,1]{0,3,2,1:T(2,128)(2,1)S(1)} %get-tuple-element.8), channel_id=1, source_target_pairs={{0,1},{1,2},{2,3},{4,5},{5,6},{6,7},{8,9},{9,10},{10,11},{12,13},{... | collective-permute-start | bytes 76808 | tf_op jit(solution)/shard_map/ppermute | solution.py:30
  296.0 2.2 collective-permute-start.11
  298.2 7.4 %collective-permute-done.11 = bf16[128,10,10,1]{0,3,2,1:T(2,128)(2,1)S(1)} collective-permute-done((bf16[128,10,10,1]{0,3,2,1:T(2,128)(2,1)S(1)}, bf16[128,10,10,1]{0,3,2,1:T(2,128)(2,1)S(1)}, u32[]{:S(2)}, u32[]{:S(2)}) %collective-permute-start.11) | collective-permute-done | bytes 25632 | tf_op jit(solution)/shard_map/ppermute | solution.py:31
  305.6 3.0 maximum_convert_fusion.1
  308.5 4.5 %fusion.19 = bf16[128,8,8,128]{0,3,2,1:T(8,128)(2,1)S(1)} fusion(f32[128,8,8,128]{0,3,2,1:T(8,128)S(1)} %copy-done, f32[128,10,10,130]{0,3,2,1:T(8,128)S(1)} %maximum_convert_fusion.1, bf16[128,8,8,128]{0,3,2,1:T(8,128)(2,1)S(1)} %get-tuple-element.24, f32[8,8,128]{2,1,0:T(8,128)S(1)} %broadcast_add_fusion), kind=kLoop, calls=%fused_computation.41 | loop fusion | flops 13631488 | bytes 33587200 | tf_op jit(solution)/shard_map/convert_element_type | solution.py:42
  313.1 3.1 collective-permute-start.12
  316.3 1.3 collective-permute-start.13
  317.6 2.0 collective-permute-done.12
  319.5 3.8 %collective-permute-done.13 = bf16[128,1,8,128]{0,3,2,1:T(8,128)(2,1)S(1)} collective-permute-done((bf16[128,1,8,128]{0,3,2,1:T(8,128)(2,1)S(1)}, bf16[128,1,8,128]{0,3,2,1:T(8,128)(2,1)S(1)}, u32[]{:S(2)}, u32[]{:S(2)}) %collective-permute-start.13) | collective-permute-done | bytes 262176 | tf_op jit(solution)/shard_map/ppermute | solution.py:31
  323.4 0.1 pad_maximum_fusion.2
  323.5 4.5 %collective-permute-start.14 = (bf16[128,10,1,128]{0,3,2,1:T(8,128)(2,1)S(1)}, bf16[128,10,1,128]{0,3,2,1:T(8,128)(2,1)S(1)}, u32[]{:S(2)}, u32[]{:S(2)}) collective-permute-start(bf16[128,10,1,128]{0,3,2,1:T(8,128)(2,1)S(1)} %get-tuple-element.12), channel_id=1, source_target_pairs={{0,4},{4,8},{8,12},{12,16},{16,20},{20,24},{24,28},{28,32},{32,36}... | collective-permute-start | bytes 983048 | tf_op jit(solution)/shard_map/ppermute | solution.py:30
  328.0 3.5 collective-permute-start.15
  331.4 5.4 %collective-permute-done.14 = bf16[128,10,1,128]{0,3,2,1:T(8,128)(2,1)S(1)} collective-permute-done((bf16[128,10,1,128]{0,3,2,1:T(8,128)(2,1)S(1)}, bf16[128,10,1,128]{0,3,2,1:T(8,128)(2,1)S(1)}, u32[]{:S(2)}, u32[]{:S(2)}) %collective-permute-start.14) | collective-permute-done | bytes 327712 | tf_op jit(solution)/shard_map/ppermute | solution.py:30
  336.8 4.5 %collective-permute-done.15 = bf16[128,10,1,128]{0,3,2,1:T(8,128)(2,1)S(1)} collective-permute-done((bf16[128,10,1,128]{0,3,2,1:T(8,128)(2,1)S(1)}, bf16[128,10,1,128]{0,3,2,1:T(8,128)(2,1)S(1)}, u32[]{:S(2)}, u32[]{:S(2)}) %collective-permute-start.15) | collective-permute-done | bytes 327712 | tf_op jit(solution)/shard_map/ppermute | solution.py:31
  341.3 0.1 pad_maximum_fusion.13
  341.4 1.9 collective-permute-start.16
  343.3 2.4 collective-permute-start.17
  345.8 6.9 %collective-permute-done.17 = bf16[128,10,10,1]{0,3,2,1:T(2,128)(2,1)S(1)} collective-permute-done((bf16[128,10,10,1]{0,3,2,1:T(2,128)(2,1)S(1)}, bf16[128,10,10,1]{0,3,2,1:T(2,128)(2,1)S(1)}, u32[]{:S(2)}, u32[]{:S(2)}) %collective-permute-start.17) | collective-permute-done | bytes 25632 | tf_op jit(solution)/shard_map/ppermute | solution.py:31
  352.7 3.0 maximum_convert_fusion.2
  355.6 4.5 %fusion.20 = bf16[128,8,8,128]{0,3,2,1:T(8,128)(2,1)S(1)} fusion(f32[128,8,8,128]{0,3,2,1:T(8,128)S(1)} %copy-done, f32[128,10,10,130]{0,3,2,1:T(8,128)S(1)} %maximum_convert_fusion.2, bf16[128,8,8,128]{0,3,2,1:T(8,128)(2,1)S(1)} %fusion.19, f32[8,8,128]{2,1,0:T(8,128)S(1)} %broadcast_add_fusion), kind=kLoop, calls=%fused_computation.42 | loop fusion | flops 13631488 | bytes 33587200 | tf_op jit(solution)/shard_map/convert_element_type | solution.py:42
  360.2 2.8 copy.22
  (15 shorter events, 0.2 us)
Async XLA Ops:
  16.3 127.5 %all-to-all-start = ((bf16[16,128,1024]{1,2,0:T(8,128)(2,1)}), bf16[16,128,1024]{1,2,0:T(8,128)(2,1)}, u32[]{:S(2)}, u32[]{:S(2)}) async-start(bf16[16,128,1024]{1,2,0:T(8,128)(2,1)} %stack.2), calls=%async_computation | async-start | bytes 8388608 | tf_op jit(solution)/shard_map/all_to_all | solution.py:15
  27.9 61.9 %copy-start.1 = (f32[8,8,128]{2,1,0:T(8,128)S(1)}, f32[8,8,128]{2,1,0:T(8,128)}, u32[]{:S(2)}) copy-start(f32[8,8,128]{2,1,0:T(8,128)} %param.8) | copy-start | bytes 98308
  27.9 187.0 %reduce-scatter.2.cloned.1.call-start = ((), (), s32[]{:S(2)}) async-start(), calls=%async_computation.3 | async-start | bytes 139264 | tf_op jit(solution)/shard_map/reduce_scatter | solution.py:68
  31.4 43.6 %collective-permute-start = (bf16[128,1,8,128]{0,3,2,1:T(8,128)(2,1)S(1)}, bf16[128,1,8,128]{0,3,2,1:T(8,128)(2,1)S(1)}, u32[]{:S(2)}, u32[]{:S(2)}) collective-permute-start(bf16[128,1,8,128]{0,3,2,1:T(8,128)(2,1)S(1)} %get-tuple-element.22), channel_id=1, source_target_pairs={{0,64},{64,128},{128,192},{1,65},{65,129},{129,193},{2,66},{66,130... | collective-permute-start | bytes 786440 | tf_op jit(solution)/shard_map/ppermute | solution.py:30
  34.6 46.3 %collective-permute-start.1 = (bf16[128,1,8,128]{0,3,2,1:T(8,128)(2,1)S(1)}, bf16[128,1,8,128]{0,3,2,1:T(8,128)(2,1)S(1)}, u32[]{:S(2)}, u32[]{:S(2)}) collective-permute-start(bf16[128,1,8,128]{0,3,2,1:T(8,128)(2,1)S(1)} %get-tuple-element.23), channel_id=1, source_target_pairs={{64,0},{128,64},{192,128},{65,1},{129,65},{193,129},{66,2},{130,66... | collective-permute-start | bytes 786440 | tf_op jit(solution)/shard_map/ppermute | solution.py:31
  81.9 44.6 %collective-permute-start.2 = (bf16[128,10,1,128]{0,3,2,1:T(8,128)(2,1)}, bf16[128,10,1,128]{0,3,2,1:T(8,128)(2,1)S(1)}, u32[]{:S(2)}, u32[]{:S(2)}) collective-permute-start(bf16[128,10,1,128]{0,3,2,1:T(8,128)(2,1)} %get-tuple-element.16), channel_id=1, source_target_pairs={{0,4},{4,8},{8,12},{12,16},{16,20},{20,24},{24,28},{28,32},{32,36}... | collective-permute-start | bytes 983048 | tf_op jit(solution)/shard_map/ppermute | solution.py:30
  83.8 51.9 %collective-permute-start.3 = (bf16[128,10,1,128]{0,3,2,1:T(8,128)(2,1)}, bf16[128,10,1,128]{0,3,2,1:T(8,128)(2,1)S(1)}, u32[]{:S(2)}, u32[]{:S(2)}) collective-permute-start(bf16[128,10,1,128]{0,3,2,1:T(8,128)(2,1)} %get-tuple-element.17), channel_id=1, source_target_pairs={{4,0},{8,4},{12,8},{16,12},{20,16},{24,20},{28,24},{32,28},{36,32}... | collective-permute-start | bytes 983048 | tf_op jit(solution)/shard_map/ppermute | solution.py:31
  135.7 97.6 %collective-permute-start.4 = (bf16[128,10,10,1]{0,3,2,1:T(2,128)(2,1)S(1)}, bf16[128,10,10,1]{0,3,2,1:T(2,128)(2,1)S(1)}, u32[]{:S(2)}, u32[]{:S(2)}) collective-permute-start(bf16[128,10,10,1]{0,3,2,1:T(2,128)(2,1)S(1)} %get-tuple-element.10), channel_id=1, source_target_pairs={{0,1},{1,2},{2,3},{4,5},{5,6},{6,7},{8,9},{9,10},{10,11},{12,13},{... | collective-permute-start | bytes 76808 | tf_op jit(solution)/shard_map/ppermute | solution.py:30
  141.9 91.5 %collective-permute-start.5 = (bf16[128,10,10,1]{0,3,2,1:T(2,128)(2,1)S(1)}, bf16[128,10,10,1]{0,3,2,1:T(2,128)(2,1)S(1)}, u32[]{:S(2)}, u32[]{:S(2)}) collective-permute-start(bf16[128,10,10,1]{0,3,2,1:T(2,128)(2,1)S(1)} %get-tuple-element.11), channel_id=1, source_target_pairs={{1,0},{2,1},{3,2},{5,4},{6,5},{7,6},{9,8},{10,9},{11,10},{13,12},{... | collective-permute-start | bytes 76808 | tf_op jit(solution)/shard_map/ppermute | solution.py:31
  216.3 24.2 %all-to-all-start.1 = ((f32[4,1,128]{2,1,0:T(1,128)}), f32[4,1,128]{2,1,0:T(1,128)}, u32[]{:S(2)}, u32[]{:S(2)}) async-start(f32[4,1,128]{2,1,0:T(1,128)} %reshape.51), calls=%async_computation.2 | async-start | bytes 4096 | tf_op jit(solution)/shard_map/all_to_all | solution.py:69
  233.4 9.1 %copy-start.2 = (s32[1,1,1,4]{3,2,1,0:T(1,128)S(1)}, s32[1,1,1,4]{3,2,1,0:T(1,128)}, u32[]{:S(2)}) copy-start(s32[1,1,1,4]{3,2,1,0:T(1,128)} %param.11) | copy-start | bytes 52
  256.6 8.2 %collective-permute-start.6 = (bf16[128,1,8,128]{0,3,2,1:T(8,128)(2,1)S(1)}, bf16[128,1,8,128]{0,3,2,1:T(8,128)(2,1)S(1)}, u32[]{:S(2)}, u32[]{:S(2)}) collective-permute-start(bf16[128,1,8,128]{0,3,2,1:T(8,128)(2,1)S(1)} %get-tuple-element.20), channel_id=1, source_target_pairs={{0,64},{64,128},{128,192},{1,65},{65,129},{129,193},{2,66},{66,130... | collective-permute-start | bytes 786440 | tf_op jit(solution)/shard_map/ppermute | solution.py:30
  259.7 8.9 %collective-permute-start.7 = (bf16[128,1,8,128]{0,3,2,1:T(8,128)(2,1)S(1)}, bf16[128,1,8,128]{0,3,2,1:T(8,128)(2,1)S(1)}, u32[]{:S(2)}, u32[]{:S(2)}) collective-permute-start(bf16[128,1,8,128]{0,3,2,1:T(8,128)(2,1)S(1)} %get-tuple-element.21), channel_id=1, source_target_pairs={{64,0},{128,64},{192,128},{65,1},{129,65},{193,129},{66,2},{130,66... | collective-permute-start | bytes 786440 | tf_op jit(solution)/shard_map/ppermute | solution.py:31
  268.7 12.2 %collective-permute-start.8 = (bf16[128,10,1,128]{0,3,2,1:T(8,128)(2,1)S(1)}, bf16[128,10,1,128]{0,3,2,1:T(8,128)(2,1)S(1)}, u32[]{:S(2)}, u32[]{:S(2)}) collective-permute-start(bf16[128,10,1,128]{0,3,2,1:T(8,128)(2,1)S(1)} %get-tuple-element.14), channel_id=1, source_target_pairs={{0,4},{4,8},{8,12},{12,16},{16,20},{20,24},{24,28},{28,32},{32,36}... | collective-permute-start | bytes 983048 | tf_op jit(solution)/shard_map/ppermute | solution.py:30
  271.6 16.8 %collective-permute-start.9 = (bf16[128,10,1,128]{0,3,2,1:T(8,128)(2,1)S(1)}, bf16[128,10,1,128]{0,3,2,1:T(8,128)(2,1)S(1)}, u32[]{:S(2)}, u32[]{:S(2)}) collective-permute-start(bf16[128,10,1,128]{0,3,2,1:T(8,128)(2,1)S(1)} %get-tuple-element.15), channel_id=1, source_target_pairs={{4,0},{8,4},{12,8},{16,12},{20,16},{24,20},{28,24},{32,28},{36,32}... | collective-permute-start | bytes 983048 | tf_op jit(solution)/shard_map/ppermute | solution.py:31
  288.4 9.7 %collective-permute-start.10 = (bf16[128,10,10,1]{0,3,2,1:T(2,128)(2,1)S(1)}, bf16[128,10,10,1]{0,3,2,1:T(2,128)(2,1)S(1)}, u32[]{:S(2)}, u32[]{:S(2)}) collective-permute-start(bf16[128,10,10,1]{0,3,2,1:T(2,128)(2,1)S(1)} %get-tuple-element.8), channel_id=1, source_target_pairs={{0,1},{1,2},{2,3},{4,5},{5,6},{6,7},{8,9},{9,10},{10,11},{12,13},{... | collective-permute-start | bytes 76808 | tf_op jit(solution)/shard_map/ppermute | solution.py:30
  295.9 12.6 %copy-start = (f32[128,8,8,128]{0,3,2,1:T(8,128)S(1)}, f32[128,8,8,128]{0,3,2,1:T(8,128)}, u32[]{:S(2)}) copy-start(f32[128,8,8,128]{0,3,2,1:T(8,128)} %get-tuple-element.25) | copy-start | bytes 12582916
  296.0 9.6 %collective-permute-start.11 = (bf16[128,10,10,1]{0,3,2,1:T(2,128)(2,1)S(1)}, bf16[128,10,10,1]{0,3,2,1:T(2,128)(2,1)S(1)}, u32[]{:S(2)}, u32[]{:S(2)}) collective-permute-start(bf16[128,10,10,1]{0,3,2,1:T(2,128)(2,1)S(1)} %get-tuple-element.9), channel_id=1, source_target_pairs={{1,0},{2,1},{3,2},{5,4},{6,5},{7,6},{9,8},{10,9},{11,10},{13,12},{... | collective-permute-start | bytes 76808 | tf_op jit(solution)/shard_map/ppermute | solution.py:31
  313.1 6.4 %collective-permute-start.12 = (bf16[128,1,8,128]{0,3,2,1:T(8,128)(2,1)S(1)}, bf16[128,1,8,128]{0,3,2,1:T(8,128)(2,1)S(1)}, u32[]{:S(2)}, u32[]{:S(2)}) collective-permute-start(bf16[128,1,8,128]{0,3,2,1:T(8,128)(2,1)S(1)} %get-tuple-element.18), channel_id=1, source_target_pairs={{0,64},{64,128},{128,192},{1,65},{65,129},{129,193},{2,66},{66,130... | collective-permute-start | bytes 786440 | tf_op jit(solution)/shard_map/ppermute | solution.py:30
  316.3 7.1 %collective-permute-start.13 = (bf16[128,1,8,128]{0,3,2,1:T(8,128)(2,1)S(1)}, bf16[128,1,8,128]{0,3,2,1:T(8,128)(2,1)S(1)}, u32[]{:S(2)}, u32[]{:S(2)}) collective-permute-start(bf16[128,1,8,128]{0,3,2,1:T(8,128)(2,1)S(1)} %get-tuple-element.19), channel_id=1, source_target_pairs={{64,0},{128,64},{192,128},{65,1},{129,65},{193,129},{66,2},{130,66... | collective-permute-start | bytes 786440 | tf_op jit(solution)/shard_map/ppermute | solution.py:31
  323.5 13.4 %collective-permute-start.14 = (bf16[128,10,1,128]{0,3,2,1:T(8,128)(2,1)S(1)}, bf16[128,10,1,128]{0,3,2,1:T(8,128)(2,1)S(1)}, u32[]{:S(2)}, u32[]{:S(2)}) collective-permute-start(bf16[128,10,1,128]{0,3,2,1:T(8,128)(2,1)S(1)} %get-tuple-element.12), channel_id=1, source_target_pairs={{0,4},{4,8},{8,12},{12,16},{16,20},{20,24},{24,28},{28,32},{32,36}... | collective-permute-start | bytes 983048 | tf_op jit(solution)/shard_map/ppermute | solution.py:30
  328.0 13.4 %collective-permute-start.15 = (bf16[128,10,1,128]{0,3,2,1:T(8,128)(2,1)S(1)}, bf16[128,10,1,128]{0,3,2,1:T(8,128)(2,1)S(1)}, u32[]{:S(2)}, u32[]{:S(2)}) collective-permute-start(bf16[128,10,1,128]{0,3,2,1:T(8,128)(2,1)S(1)} %get-tuple-element.13), channel_id=1, source_target_pairs={{4,0},{8,4},{12,8},{16,12},{20,16},{24,20},{28,24},{32,28},{36,32}... | collective-permute-start | bytes 983048 | tf_op jit(solution)/shard_map/ppermute | solution.py:31
  341.4 4.3 %collective-permute-start.16 = (bf16[128,10,10,1]{0,3,2,1:T(2,128)(2,1)S(1)}, bf16[128,10,10,1]{0,3,2,1:T(2,128)(2,1)S(1)}, u32[]{:S(2)}, u32[]{:S(2)}) collective-permute-start(bf16[128,10,10,1]{0,3,2,1:T(2,128)(2,1)S(1)} %get-tuple-element.6), channel_id=1, source_target_pairs={{0,1},{1,2},{2,3},{4,5},{5,6},{6,7},{8,9},{9,10},{10,11},{12,13},{... | collective-permute-start | bytes 76808 | tf_op jit(solution)/shard_map/ppermute | solution.py:30
  343.3 9.3 %collective-permute-start.17 = (bf16[128,10,10,1]{0,3,2,1:T(2,128)(2,1)S(1)}, bf16[128,10,10,1]{0,3,2,1:T(2,128)(2,1)S(1)}, u32[]{:S(2)}, u32[]{:S(2)}) collective-permute-start(bf16[128,10,10,1]{0,3,2,1:T(2,128)(2,1)S(1)} %get-tuple-element.7), channel_id=1, source_target_pairs={{1,0},{2,1},{3,2},{5,4},{6,5},{7,6},{9,8},{10,9},{11,10},{13,12},{... | collective-permute-start | bytes 76808 | tf_op jit(solution)/shard_map/ppermute | solution.py:31
Sparse Core Ops, SparseCore 0:
  151.7 63.1 reduce-scatter.1
